TPU v7x, 32 devices: a whole 2x2x4 slice. The times are simulated.
32 devices in a mesh: rcv: 4 (over z), src: 8 (over y, x, core).
Axes of the slice: x: 2, y: 2, z: 4, core: 2. Of those that a mesh axis runs over, the one named last changes fastest.
Arguments:
- reflection: bfloat16 [2, 16384, 16384], P(None, 'rcv', 'src'), may hold values from -6 to 6
- green: bfloat16 [2, 16384, 512], P(None, 'rcv', 'src'), may hold values from -0.046875 to 0.046875
- tile_mask: int32 [64, 64], replicated, may hold values from 0 to 1, as said below
- reference_index: int32 [512], P(('rcv', 'src')), may hold values from 0 to 511
Outputs:
- aligned: float32 [512, 2, 512], P(('rcv', 'src'))
Inputs may be any that keep to these rules, and one draw needn't show every extreme that they name: `tile_mask`: entries below the diagonal are 0.
All inputs are finite; a program needn't handle non-finite values.
Results may differ from a plain program's by a relative error of at most 0.02.
Values may be sent and summed in bfloat16 or wider, within the bound.
A program may use at most 256 MiB of HBM per device.

v0:
```python
import functools

import jax
import jax.numpy as jnp
from jax import lax
from jax.experimental import pallas as pl
from jax.experimental.pallas import tpu as pltpu
from jax.sharding import PartitionSpec as P

MESH = pl.DeviceIdType.MESH
TILE = 256
f32 = jnp.float32
bf16 = jnp.bfloat16


def dot_nn(a, b):
    return lax.dot_general(a, b, (((1,), (0,)), ((), ())), preferred_element_type=f32)


def dot_nt(a, b):
    return lax.dot_general(a, b, (((1,), (1,)), ((), ())), preferred_element_type=f32)


def kernel(
    n_rcv, n_src, mask_ref, piece_ref, refl_ref, focal_ref,
    gr, gc, y, abuf, acc, quad, slab, arrived,
    gr_send, fw_send, gr_recv, gc_send, gc_recv, gc_local, own_sem, load_sem, slab_send, slab_recv,
):
    n_dev = n_rcv * n_src
    r = lax.axis_index("rcv")
    s = lax.axis_index("src")
    me = r * n_src + s
    partner = s + 1 - 2 * lax.rem(s, 2)
    n_p, rows = gr.shape[1], gr.shape[2]
    cols = gc.shape[2]
    own_p = n_p // n_src
    out_rows = n_p // n_dev
    n_tiles = cols // TILE
    row_tiles = rows // TILE

    def last_col(src):
        return (src + 1) * cols

    def is_active(rcv, src):
        return rcv * rows < last_col(src)

    def pair_active(rcv, src):
        return rcv * rows < last_col(src - lax.rem(src, 2) + 1)

    active = is_active(r, s)
    gathers = pair_active(r, s)
    holder = (s * cols) // rows
    offset = pl.multiple_of(s * cols - holder * rows, TILE)
    on_diag = r == holder

    def load(t):
        slot = lax.rem(t, 2)
        return pltpu.make_async_copy(
            refl_ref.at[:, :, pl.ds(pl.multiple_of(t * TILE, TILE), TILE)],
            abuf.at[slot],
            load_sem.at[slot],
        )

    def gr_slot(i):
        return gr.at[:, pl.ds(pl.multiple_of(i * own_p, own_p), own_p), :]

    def gc_slot(i):
        return gc.at[:, pl.ds(pl.multiple_of(i * own_p, own_p), own_p), :]

    own_copy = pltpu.make_async_copy(piece_ref, gr_slot(s), own_sem)

    @pl.when(active)
    def _():
        load(0).start()

    @pl.when(gathers)
    def _():
        own_copy.start()

    barrier = pltpu.get_barrier_semaphore()

    @pl.loop(1, n_dev)
    def _(i):
        other = lax.rem(me + i, n_dev)
        pl.semaphore_signal(
            barrier, inc=1, device_id=(other // n_src, lax.rem(other, n_src)), device_id_type=MESH
        )

    pl.semaphore_wait(barrier, n_dev - 1)

    def piece_to(dest):
        return pltpu.make_async_remote_copy(
            src_ref=piece_ref, dst_ref=gr_slot(s), send_sem=gr_send.at[dest], recv_sem=gr_recv.at[s],
            device_id=(r, dest), device_id_type=MESH,
        )

    def forward(i):
        return pltpu.make_async_remote_copy(
            src_ref=gr_slot(i), dst_ref=gr_slot(i), send_sem=fw_send.at[i], recv_sem=gr_recv.at[i],
            device_id=(r, partner), device_id_type=MESH,
        )

    def upward(i):
        return lax.rem(i // 2, 2) == 1

    def source_target(i):
        return jnp.where(upward(i), 0, r - 1)

    def from_source(i):
        return pltpu.make_async_remote_copy(
            src_ref=gr.at[:, pl.ds(pl.multiple_of(i * own_p, own_p), own_p), pl.ds(offset, cols)],
            dst_ref=gc_slot(i), send_sem=gc_send.at[i], recv_sem=gc_recv.at[i],
            device_id=(source_target(i), s), device_id_type=MESH,
        )

    def to_local(i):
        return pltpu.make_async_copy(
            gr.at[:, pl.ds(pl.multiple_of(i * own_p, own_p), own_p), pl.ds(offset, cols)],
            gc_slot(i), gc_local.at[i],
        )

    def relay(i):
        return pltpu.make_async_remote_copy(
            src_ref=gc_slot(i), dst_ref=gc_slot(i), send_sem=gc_send.at[i], recv_sem=gc_recv.at[i],
            device_id=(jnp.where(upward(i), r + 1, r - 1), s), device_id_type=MESH,
        )

    def relays(i):
        return (jnp.logical_not(upward(i)) & (r >= 1)) | (upward(i) & (r + 1 < holder))

    def share(i):
        @pl.when(on_diag)
        def _():
            to_local(i).start()

            @pl.when(r >= 1)
            def _():
                from_source(i).start()

    same = [lax.rem(s + 2 * i, n_src) for i in range(1, n_src // 2)]
    for dest in same:
        @pl.when(pair_active(r, dest))
        def _():
            piece_to(dest).start()

    @pl.when(gathers)
    def _():
        piece_to(partner).start()
        own_copy.wait()
        share(s)
        forward(partner).wait_recv()
        share(partner)
        for i in same:
            forward(i).wait_recv()
            forward(i).start()
            share(i)
        for i in same:
            twin = i + 1 - 2 * lax.rem(i, 2)
            forward(twin).wait_recv()
            share(twin)

    per = -(-n_src // n_tiles)
    step_rows = min(rows, 1024)

    @pl.when(active)
    def _():
        @pl.loop(0, n_tiles)
        def _(t):
            slot = lax.rem(t, 2)
            load(t).wait()

            @pl.when(t + 1 < n_tiles)
            def _():
                load(t + 1).start()

            for i in range(per):
                p = t * per + i

                @pl.when((p < n_src) & jnp.logical_not(on_diag))
                def _():
                    relay(p).wait_recv()

                    @pl.when(relays(p))
                    def _():
                        relay(p).start()

            col_end = s * cols + (t + 1) * TILE
            for k in range(rows // step_rows):
                def step():
                    for j in range(step_rows // TILE):
                        m = mask_ref[k * (step_rows // TILE) + j, t]
                        at = pl.ds(k * step_rows + j * TILE, TILE)
                        for z in range(2):
                            tile = abuf[slot, z, at, :]
                            abuf[slot, z, at, :] = jnp.where(m == 1, tile, jnp.zeros_like(tile))
                    left = gr[:, :, k * step_rows:(k + 1) * step_rows].reshape(2 * n_p, step_rows)
                    for z in range(2):
                        term = dot_nn(left, abuf[slot, z, k * step_rows:(k + 1) * step_rows, :])
                        if k == 0:
                            acc[z] = term
                        else:
                            acc[z] += term

                if k == 0:
                    step()
                else:
                    pl.when(r * rows + k * step_rows < col_end)(step)
            at = pl.ds(pl.multiple_of(t * TILE, TILE), TILE)
            for z in range(2):
                y[z, :, at] = acc[z].astype(bf16)

        @pl.when(on_diag)
        def _():
            @pl.loop(0, n_src)
            def _(i):
                to_local(i).wait()

        def second(direct):
            @pl.loop(0, n_p // TILE)
            def _(b):
                at = pl.ds(pl.multiple_of(b * TILE, TILE), TILE)
                g_re = gc[0, at, :]
                g_im = gc[1, at, :]
                s_re = dot_nt(y[0, :n_p, :], g_re) + dot_nt(y[0, n_p:, :], g_im)
                k_im = dot_nt(y[1, :n_p, :], g_im) - dot_nt(y[1, n_p:, :], g_re)
                if direct:
                    quad[0, :, at] = s_re - k_im
                quad[2, :, at] = s_re + k_im
                s_im = dot_nt(y[1, :n_p, :], g_re) + dot_nt(y[1, n_p:, :], g_im)
                k_re = dot_nt(y[0, :n_p, :], g_im) - dot_nt(y[0, n_p:, :], g_re)
                if direct:
                    quad[1, :, at] = s_im + k_re
                quad[3, :, at] = s_im - k_re

        second(True)

        first_tile = s * n_tiles - r * row_tiles
        overlaps = (first_tile < row_tiles) & (first_tile + n_tiles > 0)

        @pl.when(overlaps)
        def _():
            @pl.loop(0, n_tiles)
            def _(t):
                row = first_tile + t

                @pl.when((row >= 0) & (row < row_tiles))
                def _():
                    at_r = pl.ds(pl.multiple_of(row * TILE, TILE), TILE)
                    at_c = pl.ds(pl.multiple_of(t * TILE, TILE), TILE)
                    tile_copy = pltpu.make_async_copy(
                        refl_ref.at[:, at_r, at_c], abuf.at[0, :, pl.ds(0, TILE), :], own_sem
                    )
                    tile_copy.start()
                    tile_copy.wait()
                    m = mask_ref[row, t]
                    left = gr[:, :, at_r].reshape(2 * n_p, TILE)
                    for z in range(2):
                        tile = abuf[0, z, :TILE, :]
                        tile = jnp.where(m == 1, tile, jnp.zeros_like(tile))
                        kept = y[z, :, at_c].astype(f32) - dot_nn(left, tile)
                        y[z, :, at_c] = kept.astype(bf16)

            second(False)

        for part in range(2):
            for b in range(n_p // TILE):
                turned = quad[2 + part, :, b * TILE:(b + 1) * TILE].T
                quad[part, b * TILE:(b + 1) * TILE, :] += turned

        group = max(16, out_rows)

        @pl.loop(0, n_p // group)
        def _(g):
            at = pl.ds(pl.multiple_of(g * group, group), group)
            for part in range(2):
                block = quad[part, at, :]
                for j in range(group // out_rows):
                    slab[g * (group // out_rows) + j, :, part * n_p:(part + 1) * n_p] = block[
                        j * out_rows:(j + 1) * out_rows
                    ].astype(bf16)

    def slab_to(other):
        return pltpu.make_async_remote_copy(
            src_ref=slab.at[other], dst_ref=arrived.at[me], send_sem=slab_send.at[other],
            recv_sem=slab_recv.at[me],
            device_id=(other // n_src, lax.rem(other, n_src)), device_id_type=MESH,
        )

    def slab_from(other):
        return pltpu.make_async_remote_copy(
            src_ref=slab.at[me], dst_ref=arrived.at[other], send_sem=slab_send.at[other],
            recv_sem=slab_recv.at[other],
            device_id=(other // n_src, lax.rem(other, n_src)), device_id_type=MESH,
        )

    @pl.when(active)
    def _():
        @pl.loop(1, n_dev)
        def _(i):
            slab_to(lax.rem(me + i, n_dev)).start()

    focal_ref[...] = jnp.zeros_like(focal_ref)

    @pl.when(active)
    def _():
        focal_ref[...] = slab[me].astype(f32)

    for other in range(n_dev):
        if (other // n_src) * rows < (other % n_src + 1) * cols:
            @pl.when(me != other)
            def _():
                slab_from(other).wait_recv()
                focal_ref[...] += arrived[other].astype(f32)

    @pl.when(active)
    def _():
        @pl.loop(1, n_dev)
        def _(i):
            slab_to(lax.rem(me + i, n_dev)).wait_send()

    for dest in same:
        @pl.when(pair_active(r, dest))
        def _():
            piece_to(dest).wait_send()

    @pl.when(gathers)
    def _():
        piece_to(partner).wait_send()
        for i in same:
            forward(i).wait_send()

        @pl.loop(0, n_src)
        def _(i):
            @pl.when(on_diag & (r >= 1))
            def _():
                from_source(i).wait_send()

            @pl.when(active & jnp.logical_not(on_diag) & relays(i))
            def _():
                relay(i).wait_send()


def body(reflection, green, tile_mask, reference_index):
    rows, cols = reflection.shape[1], reflection.shape[2]
    n_rcv, n_src = lax.axis_size("rcv"), lax.axis_size("src")
    n_dev = n_rcv * n_src
    own_p = green.shape[2]
    n_p = own_p * n_src
    out_rows = n_p // n_dev
    r, s = lax.axis_index("rcv"), lax.axis_index("src")
    row_tiles, n_tiles = rows // TILE, cols // TILE
    tile_block = lax.dynamic_slice(tile_mask, (r * row_tiles, s * n_tiles), (row_tiles, n_tiles))
    piece = jnp.swapaxes(green, 1, 2)
    dma = pltpu.SemaphoreType.DMA
    any_spec = pl.BlockSpec(memory_space=pl.ANY)
    focal = pl.pallas_call(
        functools.partial(kernel, n_rcv, n_src),
        out_shape=jax.ShapeDtypeStruct((out_rows, 2 * n_p), f32),
        in_specs=[pl.BlockSpec(memory_space=pltpu.SMEM), any_spec, any_spec],
        out_specs=pl.BlockSpec(memory_space=pltpu.VMEM),
        scratch_shapes=[
            pltpu.VMEM((2, n_p, rows), bf16),
            pltpu.VMEM((2, n_p, cols), bf16),
            pltpu.VMEM((2, 2 * n_p, cols), bf16),
            pltpu.VMEM((2, 2, rows, TILE), bf16),
            pltpu.VMEM((2, 2 * n_p, TILE), f32),
            pltpu.VMEM((4, n_p, n_p), f32),
            pltpu.VMEM((n_dev, out_rows, 2 * n_p), bf16),
            pltpu.VMEM((n_dev, out_rows, 2 * n_p), bf16),
            dma((n_src,)), dma((n_src,)), dma((n_src,)), dma((n_src,)), dma((n_src,)), dma((n_src,)),
            dma, dma((2,)), dma((n_dev,)), dma((n_dev,)),
        ],
        compiler_params=pltpu.CompilerParams(
            collective_id=0, has_side_effects=True, vmem_limit_bytes=60 * 1024 * 1024
        ),
        name="focus",
    )(tile_block, piece, reflection)
    focal_real = focal[:, :n_p]
    focal_imag = focal[:, n_p:]
    chosen = jnp.arange(n_p)[None, :] == reference_index[:, None]
    anchor_real = jnp.sum(jnp.where(chosen, focal_real, 0.0), axis=1)[:, None]
    anchor_imag = jnp.sum(jnp.where(chosen, focal_imag, 0.0), axis=1)[:, None]
    out_real = focal_real * anchor_real + focal_imag * anchor_imag
    out_imag = focal_imag * anchor_real - focal_real * anchor_imag
    return jnp.stack([out_real, out_imag], axis=1)


def solution(mesh):
    return jax.shard_map(
        body,
        mesh=mesh,
        in_specs=(P(None, "rcv", "src"), P(None, "rcv", "src"), P(), P(("rcv", "src"))),
        out_specs=P(("rcv", "src"), None, None),
        check_vma=False,
    )
```

profile of v0, /device:TPU:13, one launch (start us, length us, event | category | flops | bytes accessed | tf_op | source)
XLA Modules:
  0.0 282.9 jit_solution(10046186792850499356)
XLA Ops:
  0.0 0.0 copy-start
  0.0 1.4 dynamic_slice.3.mask_ref
  1.4 278.9 %focus.1 = f32[16,1024]{1,0:T(8,128)} custom-call(s32[16,8]{1,0:T(8,128)} %dynamic_slice.3.mask_ref, bf16[2,64,4096]{2,1,0:T(8,128)(2,1)} %bitcast.5, bf16[2,4096,2048]{2,1,0:T(8,128)(2,1)} %refl_ref.1), custom_call_target="tpu_custom_call" | custom-call | tf_op jit(solution)/shard_map/focus/pallas_call | solution.py:356
  280.3 0.0 copy-done
  280.3 1.0 select_reduce_fusion.1
  281.3 0.9 add_bitcast_fusion
  282.2 0.7 copy.5
  (1 shorter events, 0.0 us)
Async XLA Ops:
  0.0 280.3 %copy-start = (s32[16]{0:T(128)S(1)}, s32[16]{0:T(128)}, u32[]{:S(2)}) copy-start(s32[16]{0:T(128)} %param.7) | copy-start | bytes 196
where the time goes:
time: 284 us; the launch traced here: 283 us
  Pallas kernels  279 us (98%)
    pallas_call x1, Pallas kernels, body(): pl.pallas_call(functools.partial(kernel, n_rcv, n_src), out_shape=jax.Sha...  279 us

commit v1 on v0

v1 whole, which is shorter than its diff:
```python
import functools

import jax
import jax.numpy as jnp
from jax import lax
from jax.experimental import pallas as pl
from jax.experimental.pallas import tpu as pltpu
from jax.sharding import PartitionSpec as P

MESH = pl.DeviceIdType.MESH
TILE = 256
f32 = jnp.float32
bf16 = jnp.bfloat16


def dot_nn(a, b):
    return lax.dot_general(a, b, (((1,), (0,)), ((), ())), preferred_element_type=f32)


def dot_nt(a, b):
    return lax.dot_general(a, b, (((1,), (1,)), ((), ())), preferred_element_type=f32)


class Plan:
    def __init__(self, n):
        self.n = n
        self.row = {}
        self.col = {}
        self.relay = {}
        self.down = {}
        self.passes = [{}, {}, {}]
        self.order = {}
        chips = [(z, c) for z in range(n) for c in range(n)]
        for z, c in chips:
            self.row[z, c] = []
            self.col[z, c] = []
            self.order[z, c] = list(range(n))
        if n == 4:
            self.plan_4()
        else:
            for z, c in chips:
                self.row[z, c] = [t for t in sorted(range(z, n), key=lambda t: t ^ c) if t != c]
                self.col[z, c] = [(t, z, c) for t in range(z)]
        waited = {chip: {op[0] for stage in self.passes for op in stage.get(chip, []) if op[4]} for chip in chips}
        self.waits = {chip: [int(q not in waited[chip]) for q in self.order[chip]] for chip in chips}

    def plan_4(self):
        via = {0: 2, 1: 3, 2: 3, 3: 1}
        for z in range(4):
            for q in range(4):
                for j in (1, 2, 3):
                    t = q ^ j
                    if t < z:
                        continue
                    hop = via[q]
                    if j < 3 or hop < z or (z == 2 and q == 0) or z == 3:
                        self.row[z, q].append(t)
                    else:
                        self.relay.setdefault(((z, hop), hop ^ q), []).append(t)
        col = self.col
        for b in (1, 2, 3):
            col[b, b].append((0, b, b))
        col[1, 0].append((0, 1, 0))
        col[2, 0].append((1, 0, 2))
        col[3, 0].append((1, 0, 3))
        col[2, 1].append((1, 2, 1))
        col[3, 1].append((1, 3, 1))
        col[3, 0].append((2, 3, 0))
        col[3, 2].append((2, 3, 2))
        col[3, 3].append((3, 2, 3))
        for b in (1, 2, 3):
            for q in (1, 2, 3):
                if q != b:
                    self.down[(b, b), b ^ q] = [0]
        a, b, _ = self.passes
        a[1, 0] = [(2, 0, 2, 0, 1), (3, 0, 3, 0, 1), (2, 1, 2, 0, 0), (3, 1, 3, 0, 0)]
        a[3, 2] = [(3, 2, 3, 3, 1)]
        a[0, 2] = [(2, 1, 2, 2, 1)]
        a[0, 3] = [(3, 1, 3, 3, 1)]
        b[0, 2] = [(3, 1, 2, 3, 1)]
        b[0, 3] = [(2, 1, 3, 2, 1)]
        b[1, 3] = [(1, 2, 3, 1, 1)]
        order = self.order
        order[0, 1] = [1, 3, 0, 2]
        order[0, 2] = [2, 3, 0, 1]
        order[0, 3] = [3, 2, 0, 1]
        order[1, 2] = [2, 1, 0, 3]
        order[1, 3] = [1, 3, 0, 2]
        order[2, 3] = [2, 0, 3, 1]

    def table(self, get):
        n = self.n
        return [get((i // n, i % n)) for i in range(n * n)]


def xor(a, b, n):
    out, bit = 0, 1
    while bit < n:
        out = out + bit * lax.rem(a // bit + b // bit, 2)
        bit *= 2
    return out


def kernel(
    n_rcv, n_src, mask_ref, piece_ref, refl_ref, focal_ref,
    a_buf, gr, gc, y, acc, focal, slab, arrived,
    load_sem, own_sem, row_send, pass_send, relay_send, gr_recv,
    col_send, down_send, step_send, gc_recv, gc_local, slab_send, slab_recv,
):
    n_dev = n_rcv * n_src
    n = n_src // 2
    plan = Plan(n)
    r = lax.axis_index("rcv")
    s = lax.axis_index("src")
    me = r * n_src + s
    c = s // 2
    h = lax.rem(s, 2)
    chip = r * n + c
    own_p, rows = gr.shape[2], gr.shape[3]
    n_p = own_p * n_src
    cols = gc.shape[3]
    out_rows = n_p // n_dev
    quarter = 2 * own_p
    n_tiles, row_tiles = cols // TILE, rows // TILE
    user = c >= r
    on_diag = c == r
    full = c > r

    def look(get, default=0):
        value = jnp.int32(default)
        for i, entry in enumerate(plan.table(get)):
            if entry != default:
                value = jnp.where(chip == i, entry, value)
        return value

    def width(lists):
        return max([len(ops) for ops in lists.values()] + [0])

    def entry(lists, i, field=None, default=-1):
        def get(key):
            ops = lists.get(key, [])
            if i >= len(ops):
                return default
            return ops[i] if field is None else ops[i][field]

        return get

    def load(t):
        return pltpu.make_async_copy(
            refl_ref.at[:, :, pl.ds(t * TILE, TILE)], a_buf.at[t], load_sem.at[t]
        )

    own_copy = pltpu.make_async_copy(piece_ref, gr.at[h], own_sem)

    @pl.when(user)
    def _():
        own_copy.start()
        for t in range(n_tiles):
            load(t).start()

    barrier = pltpu.get_barrier_semaphore()

    @pl.loop(1, n_dev)
    def _(i):
        other = lax.rem(me + i, n_dev)
        pl.semaphore_signal(
            barrier, inc=1, device_id=(other // n_src, lax.rem(other, n_src)), device_id_type=MESH
        )

    pl.semaphore_wait(barrier, n_dev - 1)

    def row_to(i):
        to = look(entry(plan.row, i))
        slot = 2 * xor(c, to, n) + h
        return to >= 0, pltpu.make_async_remote_copy(
            src_ref=piece_ref, dst_ref=gr.at[slot], send_sem=row_send.at[i], recv_sem=gr_recv.at[slot],
            device_id=(r, 2 * to + h), device_id_type=MESH,
        )

    def to_partner(j):
        slot = 2 * j + h
        src = piece_ref if j == 0 else gr.at[slot]
        return pltpu.make_async_remote_copy(
            src_ref=src, dst_ref=gr.at[slot], send_sem=pass_send.at[j], recv_sem=gr_recv.at[slot],
            device_id=(r, 2 * c + 1 - h), device_id_type=MESH,
        )

    def arrival(slot):
        return pltpu.make_async_remote_copy(
            src_ref=piece_ref, dst_ref=gr.at[slot], send_sem=pass_send.at[0], recv_sem=gr_recv.at[slot],
            device_id=(r, 2 * c + 1 - h), device_id_type=MESH,
        )

    def relay_to(j, i):
        lists = {key[0]: ops for key, ops in plan.relay.items() if key[1] == j}
        to = look(entry(lists, i))
        slot = 2 * j + h
        there = 2 * xor(xor(c, j, n), to, n) + h
        return to >= 0, pltpu.make_async_remote_copy(
            src_ref=gr.at[slot], dst_ref=gr.at[there], send_sem=relay_send.at[j, i],
            recv_sem=gr_recv.at[there], device_id=(r, 2 * to + h), device_id_type=MESH,
        )

    def relays(j):
        return width({key: ops for key, ops in plan.relay.items() if key[1] == j})

    def col_part(ref_slot, half):
        return gc.at[ref_slot, :, pl.ds(pl.multiple_of(half * own_p, own_p), own_p), :]

    def col_to(i, k):
        z = look(entry(plan.col, i, 0))
        to = look(entry(plan.col, i, 1))
        slot = look(entry(plan.col, i, 2))
        return z >= 0, pltpu.make_async_remote_copy(
            src_ref=piece_ref.at[:, :, pl.ds(k * cols, cols)], dst_ref=col_part(slot, h),
            send_sem=col_send.at[i, k], recv_sem=gc_recv.at[2 * slot + h],
            device_id=(z, 2 * to + k), device_id_type=MESH,
        )

    def down_to(j, i, half):
        lists = {key[0]: ops for key, ops in plan.down.items() if key[1] == j}
        z = look(entry(lists, i))
        q = xor(c, j, n)
        return z >= 0, pltpu.make_async_remote_copy(
            src_ref=gr.at[2 * j + half, :, :, pl.ds(pl.multiple_of(h * cols, cols), cols)],
            dst_ref=col_part(q, half), send_sem=down_send.at[j, i, half], recv_sem=gc_recv.at[2 * q + half],
            device_id=(z, s), device_id_type=MESH,
        )

    def downs(j):
        return width({key: ops for key, ops in plan.down.items() if key[1] == j})

    def step_to(stage, i, half):
        lists = plan.passes[stage]
        slot = look(entry(lists, i, 0))
        there = look(entry(lists, i, 3))
        return slot >= 0, look(entry(lists, i, 4)) == 1, slot, pltpu.make_async_remote_copy(
            src_ref=col_part(slot, half), dst_ref=col_part(there, half),
            send_sem=step_send.at[stage, i, half], recv_sem=gc_recv.at[2 * there + half],
            device_id=(look(entry(lists, i, 1)), 2 * look(entry(lists, i, 2)) + h), device_id_type=MESH,
        )

    def col_arrival(slot, half):
        return pltpu.make_async_remote_copy(
            src_ref=piece_ref.at[:, :, pl.ds(0, cols)], dst_ref=col_part(slot, half),
            send_sem=col_send.at[0, 0], recv_sem=gc_recv.at[2 * slot + half],
            device_id=(r, 2 * c + 1 - h), device_id_type=MESH,
        )

    def to_local(j, half):
        q = xor(c, j, n)
        return pltpu.make_async_copy(
            gr.at[2 * j + half, :, :, pl.ds(pl.multiple_of(h * cols, cols), cols)],
            col_part(q, half), gc_local.at[j, half],
        )

    def pass_on(stage):
        for i in range(width(plan.passes[stage])):
            for half in range(2):
                valid, waits, slot, copy = step_to(stage, i, half)

                @pl.when(valid)
                def _():
                    @pl.when(waits)
                    def _():
                        col_arrival(slot, half).wait_recv()

                    copy.start()

    @pl.when(user)
    def _():
        to_partner(0).start()

    for i in range(width(plan.row)):
        valid, copy = row_to(i)
        pl.when(valid)(copy.start)
    for i in range(width(plan.col)):
        for k in range(2):
            valid, copy = col_to(i, k)
            pl.when(valid)(copy.start)

    @pl.when(user)
    def _():
        own_copy.wait()

    def take(j):
        @pl.when(user)
        def _():
            arrival(2 * j + h).wait_recv()
            to_partner(j).start()
            for i in range(relays(j)):
                valid, copy = relay_to(j, i)
                pl.when(valid)(copy.start)

    def twin(j):
        @pl.when(user)
        def _():
            arrival(2 * j + 1 - h).wait_recv()
            for half in range(2):
                for i in range(downs(j)):
                    valid, copy = down_to(j, i, half)
                    pl.when(valid)(copy.start)

                @pl.when(on_diag)
                def _():
                    to_local(j, half).start()

    step_rows = min(rows, 1024)
    step_tiles = step_rows // TILE

    def clean(t, first, count):
        for j in range(first, first + count):
            m = mask_ref[j, t]
            at = pl.ds(j * TILE, TILE)
            for z in range(2):
                tile = a_buf[t, z, at, :]
                a_buf[t, z, at, :] = jnp.where(m == 1, tile, jnp.zeros_like(tile))

    def focal_rows(j, half):
        return pl.ds(pl.multiple_of(xor(c, j, n) * quarter + half * own_p, own_p), own_p)

    def keep(z, t, j0, nj, block):
        at = pl.ds(pl.multiple_of(t * TILE, TILE), TILE)
        block = block.astype(bf16)
        for j in range(nj):
            for half in range(2):
                for part in range(2):
                    start = ((j * 2 + half) * 2 + part) * own_p
                    y[z, part, focal_rows(j0 + j, half), at] = block[start:start + own_p]

    def first(j0, nj):
        m_rows = nj * 2 * quarter

        @pl.when(full)
        def _():
            @pl.loop(0, n_tiles)
            def _(t):
                if j0 == 0:
                    load(t).wait()
                    clean(t, 0, row_tiles)
                left = gr[2 * j0:2 * (j0 + nj)].reshape(m_rows, rows)
                for z in range(2):
                    keep(z, t, j0, nj, dot_nn(left, a_buf[t, z]))

        @pl.when(on_diag)
        def _():
            @pl.loop(0, n_tiles)
            def _(t):
                if j0 == 0:
                    load(t).wait()
                    clean(t, 0, row_tiles)
                col_end = h * cols + (t + 1) * TILE
                for k in range(rows // step_rows):
                    def step():
                        left = gr[2 * j0:2 * (j0 + nj), :, :, k * step_rows:(k + 1) * step_rows]
                        left = left.reshape(m_rows, step_rows)
                        for z in range(2):
                            term = dot_nn(left, a_buf[t, z, k * step_rows:(k + 1) * step_rows, :])
                            if k == 0:
                                acc[z, :m_rows] = term
                            else:
                                acc[z, :m_rows] += term

                    if k == 0:
                        step()
                    else:
                        pl.when(k * step_rows < col_end)(step)
                for z in range(2):
                    keep(z, t, j0, nj, acc[z, :m_rows])

    unit = max(quarter, 128)
    per = unit // quarter

    def second(i, direct, mirror):
        g = jnp.concatenate([gc[i * per + k, part] for part in range(2) for k in range(per)], axis=0)
        here = pl.ds(pl.multiple_of(i * unit, unit), unit)
        sums, turns = [], []
        for z in range(2):
            by_re = dot_nt(y[z, 0], g)
            by_im = dot_nt(y[z, 1], g)
            sums.append(by_re[:, :unit] + by_im[:, unit:])
            turns.append(by_re[:, unit:] - by_im[:, :unit])
        for part in range(2):
            turn = turns[0] if part else -turns[1]
            if direct:
                focal[part, :, here] += sums[part] + turn
            if mirror:
                focal[part, here, :] += (sums[part] - turn).T

    groups = [[0], [1, 2]] + ([list(range(3, n))] if n > 3 else [])
    for stage, group in enumerate(groups):
        if stage:
            for j in group:
                take(j)
        if stage:
            pass_on(stage - 1)
        for j in group:
            twin(j)
        first(group[0], len(group))

    for part in range(2):
        @pl.when(user)
        def _():
            focal[part] = jnp.zeros_like(focal[part])

    @pl.when(full)
    def _():
        @pl.loop(0, n // per)
        def _(i):
            slot = jnp.int32(0)
            waits = jnp.bool_(False)
            for k in range(n // per):
                slot = jnp.where(i == k, look(lambda key: plan.order[key][k]), slot)
                waits = waits | ((i == k) & (look(lambda key: plan.waits[key][k], 1) == 1))

            @pl.when(waits)
            def _():
                for k in range(per):
                    col_arrival(slot * per + k, 0).wait_recv()
                    col_arrival(slot * per + k, 1).wait_recv()

            second(slot, True, True)

    @pl.when(on_diag)
    def _():
        for j in range(n):
            for half in range(2):
                to_local(j, half).wait()

        @pl.loop(0, n // per)
        def _(q):
            second(q, True, False)

        @pl.loop(0, n_tiles)
        def _(t):
            row = h * n_tiles + t
            at_r = pl.ds(pl.multiple_of(row * TILE, TILE), TILE)
            at_c = pl.ds(pl.multiple_of(t * TILE, TILE), TILE)
            left = gr[:, :, :, at_r].reshape(2 * n_p, TILE)
            for z in range(2):
                term = dot_nn(left, a_buf[t, z, at_r, :])
                for j in range(n_src):
                    for part in range(2):
                        at_p = focal_rows(j // 2, j % 2)
                        start = (j * 2 + part) * own_p
                        kept = y[z, part, at_p, at_c].astype(f32) - term[start:start + own_p]
                        y[z, part, at_p, at_c] = kept.astype(bf16)

        @pl.loop(0, n // per)
        def _(q):
            second(q, False, True)

    @pl.when(user)
    def _():
        group = max(16, out_rows)

        @pl.loop(0, n_p // group)
        def _(g):
            at = pl.ds(pl.multiple_of(g * group, group), group)
            for part in range(2):
                block = focal[part, at, :]
                for j in range(group // out_rows):
                    slab[g * (group // out_rows) + j, :, part * n_p:(part + 1) * n_p] = block[
                        j * out_rows:(j + 1) * out_rows
                    ].astype(bf16)

    def slab_to(other):
        return pltpu.make_async_remote_copy(
            src_ref=slab.at[other], dst_ref=arrived.at[me], send_sem=slab_send.at[other],
            recv_sem=slab_recv.at[me],
            device_id=(other // n_src, lax.rem(other, n_src)), device_id_type=MESH,
        )

    def slab_from(other):
        return pltpu.make_async_remote_copy(
            src_ref=slab.at[me], dst_ref=arrived.at[other], send_sem=slab_send.at[other],
            recv_sem=slab_recv.at[other],
            device_id=(other // n_src, lax.rem(other, n_src)), device_id_type=MESH,
        )

    @pl.when(user)
    def _():
        @pl.loop(1, n_dev)
        def _(i):
            slab_to(lax.rem(me + i, n_dev)).start()

    focal_ref[...] = jnp.zeros_like(focal_ref)

    @pl.when(user)
    def _():
        focal_ref[...] = slab[me].astype(f32)

    for other in range(n_dev):
        if (other % n_src) // 2 >= other // n_src:
            @pl.when(me != other)
            def _():
                slab_from(other).wait_recv()
                focal_ref[...] += arrived[other].astype(f32)

    @pl.when(user)
    def _():
        @pl.loop(1, n_dev)
        def _(i):
            slab_to(lax.rem(me + i, n_dev)).wait_send()

    for i in range(width(plan.row)):
        valid, copy = row_to(i)
        pl.when(valid)(copy.wait_send)
    for i in range(width(plan.col)):
        for k in range(2):
            valid, copy = col_to(i, k)
            pl.when(valid)(copy.wait_send)
    for stage in range(len(plan.passes)):
        for i in range(width(plan.passes[stage])):
            for half in range(2):
                valid, _, _, copy = step_to(stage, i, half)
                pl.when(valid)(copy.wait_send)

    @pl.when(user)
    def _():
        for j in range(n):
            to_partner(j).wait_send()
            for i in range(relays(j)):
                valid, copy = relay_to(j, i)
                pl.when(valid)(copy.wait_send)
            for half in range(2):
                for i in range(downs(j)):
                    valid, copy = down_to(j, i, half)
                    pl.when(valid)(copy.wait_send)


def body(reflection, green, tile_mask, reference_index):
    rows, cols = reflection.shape[1], reflection.shape[2]
    n_rcv, n_src = lax.axis_size("rcv"), lax.axis_size("src")
    n_dev = n_rcv * n_src
    own_p = green.shape[2]
    n_p = own_p * n_src
    out_rows = n_p // n_dev
    n = n_src // 2
    assert n == n_rcv and rows == 2 * cols
    r, s = lax.axis_index("rcv"), lax.axis_index("src")
    row_tiles, n_tiles = rows // TILE, cols // TILE
    tile_block = lax.dynamic_slice(tile_mask, (r * row_tiles, s * n_tiles), (row_tiles, n_tiles))
    piece = jnp.swapaxes(green, 1, 2)
    dma = pltpu.SemaphoreType.DMA
    any_spec = pl.BlockSpec(memory_space=pl.ANY)
    focal = pl.pallas_call(
        functools.partial(kernel, n_rcv, n_src),
        out_shape=jax.ShapeDtypeStruct((out_rows, 2 * n_p), f32),
        in_specs=[pl.BlockSpec(memory_space=pltpu.SMEM), any_spec, any_spec],
        out_specs=pl.BlockSpec(memory_space=pltpu.VMEM),
        scratch_shapes=[
            pltpu.VMEM((n_tiles, 2, rows, TILE), bf16),
            pltpu.VMEM((n_src, 2, own_p, rows), bf16),
            pltpu.VMEM((n, 2, 2 * own_p, cols), bf16),
            pltpu.VMEM((2, 2, n_p, cols), bf16),
            pltpu.VMEM((2, 4 * own_p * max(2, n - 3), TILE), f32),
            pltpu.VMEM((2, n_p, n_p), f32),
            pltpu.VMEM((n_dev, out_rows, 2 * n_p), bf16),
            pltpu.VMEM((n_dev, out_rows, 2 * n_p), bf16),
            dma((n_tiles,)), dma, dma((n,)), dma((n,)), dma((n, 2)), dma((n_src,)),
            dma((n, 2)), dma((n, 1, 2)), dma((3, 4, 2)), dma((n_src,)), dma((n, 2)), dma((n_dev,)), dma((n_dev,)),
        ],
        compiler_params=pltpu.CompilerParams(
            collective_id=0, has_side_effects=True, vmem_limit_bytes=63 * 1024 * 1024
        ),
        name="focus",
    )(tile_block, piece, reflection)
    focal_real = focal[:, :n_p]
    focal_imag = focal[:, n_p:]
    chosen = jnp.arange(n_p)[None, :] == reference_index[:, None]
    anchor_real = jnp.sum(jnp.where(chosen, focal_real, 0.0), axis=1)[:, None]
    anchor_imag = jnp.sum(jnp.where(chosen, focal_imag, 0.0), axis=1)[:, None]
    out_real = focal_real * anchor_real + focal_imag * anchor_imag
    out_imag = focal_imag * anchor_real - focal_real * anchor_imag
    return jnp.stack([out_real, out_imag], axis=1)


def solution(mesh):
    return jax.shard_map(
        body,
        mesh=mesh,
        in_specs=(P(None, "rcv", "src"), P(None, "rcv", "src"), P(), P(("rcv", "src"))),
        out_specs=P(("rcv", "src"), None, None),
        check_vma=False,
    )
```

time: 284 us -> 154 us (0.54)
  Pallas kernels: 279 us -> 150 us
    pallas_call x1, Pallas kernels: 279 us -> 150 us  [body(): pl.pallas_call(functools.partial(kernel, n_rcv, n_src), out_shape=jax.Sha...]
where the time goes in v1:
time: 154 us; the launch traced here: 153 us
  Pallas kernels  150 us (97%)
  local copies, waits for them, and re-layouts  2.07 us (1%)
  other arithmetic  1.82 us (1%)
    pallas_call x1, Pallas kernels, body(): pl.pallas_call(functools.partial(kernel, n_rcv, n_src), out_shape=jax.Sha...  150 us

profile of v1, /device:TPU:13, one launch (start us, length us, event | category | flops | bytes accessed | tf_op | source)
XLA Modules:
  0.0 153.4 jit_solution(4257147814671721801)
XLA Ops:
  0.0 0.0 copy-start
  0.0 1.4 dynamic_slice.3.mask_ref
  1.4 149.5 %focus.1 = f32[16,1024]{1,0:T(8,128)} custom-call(s32[16,8]{1,0:T(8,128)} %dynamic_slice.3.mask_ref, bf16[2,64,4096]{2,1,0:T(8,128)(2,1)} %bitcast.5, bf16[2,4096,2048]{2,1,0:T(8,128)(2,1)} %refl_ref.1), custom_call_target="tpu_custom_call" | custom-call | tf_op jit(solution)/shard_map/focus/pallas_call | solution.py:547
  150.9 0.0 copy-done
  150.9 1.0 select_reduce_fusion.1
  151.9 0.9 add_bitcast_fusion
  152.8 0.7 copy.5
  (1 shorter events, 0.0 us)
Async XLA Ops:
  0.0 150.9 %copy-start = (s32[16]{0:T(128)S(1)}, s32[16]{0:T(128)}, u32[]{:S(2)}) copy-start(s32[16]{0:T(128)} %param.7) | copy-start | bytes 196

commit v2 on v1

--- a/solution.py
+++ b/solution.py
@@ -21,72 +21,46 @@
     return lax.dot_general(a, b, (((1,), (1,)), ((), ())), preferred_element_type=f32)
 
 
+ROW = [
+    {(0, 0): [1, 2], (0, 1): [0, 3], (0, 2): [3, 0], (0, 3): [2, 1], (1, 0): [1, 2], (1, 1): [3], (1, 2): [3], (1, 3): [2, 1], (2, 0): [2, 3], (2, 1): [3, 2], (2, 2): [3], (2, 3): [2], (3, 0): [3], (3, 1): [3], (3, 2): [3]},
+    {},
+    {},
+]
+COL = [
+    {(1, 0): [(0, 1, 0)], (1, 1): [(0, 1, 1)], (2, 0): [(1, 0, 0)], (2, 1): [(1, 2, 1)], (2, 2): [(0, 2, 2)], (3, 0): [(1, 0, 1), (2, 3, 0)], (3, 1): [(1, 3, 1)], (3, 2): [(2, 3, 2)], (3, 3): [(0, 3, 3), (3, 2, 0)]},
+    {},
+    {},
+]
+RELAY = {((0, 1), 2): [0], ((0, 2), 2): [3], ((0, 3), 2): [2], ((0, 3), 1): [1], ((1, 2), 2): [3], ((1, 3), 2): [2], ((1, 3), 1): [1]}
+DOWN = {((1, 1), 3): [0], ((1, 1), 2): [0], ((2, 2), 3): [0], ((2, 2), 1): [0], ((3, 3), 2): [0], ((3, 3), 1): [0]}
+STEP = [
+    {(0, 2): [(2, 1, 2, 2, 1)], (0, 3): [(3, 1, 3, 3, 1)], (1, 0): [(0, 0, 2, 0, 1), (0, 1, 2, 0, 0), (1, 0, 3, 0, 1), (1, 1, 3, 0, 0)], (3, 2): [(0, 2, 3, 3, 1)]},
+    {(0, 2): [(3, 1, 2, 3, 1)], (0, 3): [(2, 1, 3, 2, 1)], (1, 3): [(1, 2, 3, 1, 1)]},
+    {},
+]
+ORDER = {(0, 1): [1, 0, 3, 2], (0, 2): [2, 3, 0, 1], (0, 3): [3, 2, 1, 0], (1, 2): [1, 2, 0, 3], (1, 3): [3, 1, 0, 2], (2, 3): [2, 0, 3, 1]}
+
+
 class Plan:
     def __init__(self, n):
         self.n = n
-        self.row = {}
-        self.col = {}
-        self.relay = {}
-        self.down = {}
-        self.passes = [{}, {}, {}]
-        self.order = {}
+        self.row, self.col, self.step = ([{}, {}, {}] for _ in range(3))
+        self.relay, self.down, self.order = {}, {}, {}
         chips = [(z, c) for z in range(n) for c in range(n)]
-        for z, c in chips:
-            self.row[z, c] = []
-            self.col[z, c] = []
-            self.order[z, c] = list(range(n))
         if n == 4:
-            self.plan_4()
+            for point in range(3):
+                self.row[point] = ROW[point]
+                self.col[point] = COL[point]
+                self.step[point] = STEP[point]
+            self.relay, self.down, self.order = RELAY, DOWN, ORDER
         else:
             for z, c in chips:
-                self.row[z, c] = [t for t in sorted(range(z, n), key=lambda t: t ^ c) if t != c]
-                self.col[z, c] = [(t, z, c) for t in range(z)]
-        waited = {chip: {op[0] for stage in self.passes for op in stage.get(chip, []) if op[4]} for chip in chips}
-        self.waits = {chip: [int(q not in waited[chip]) for q in self.order[chip]] for chip in chips}
-
-    def plan_4(self):
-        via = {0: 2, 1: 3, 2: 3, 3: 1}
-        for z in range(4):
-            for q in range(4):
-                for j in (1, 2, 3):
-                    t = q ^ j
-                    if t < z:
-                        continue
-                    hop = via[q]
-                    if j < 3 or hop < z or (z == 2 and q == 0) or z == 3:
-                        self.row[z, q].append(t)
-                    else:
-                        self.relay.setdefault(((z, hop), hop ^ q), []).append(t)
-        col = self.col
-        for b in (1, 2, 3):
-            col[b, b].append((0, b, b))
-        col[1, 0].append((0, 1, 0))
-        col[2, 0].append((1, 0, 2))
-        col[3, 0].append((1, 0, 3))
-        col[2, 1].append((1, 2, 1))
-        col[3, 1].append((1, 3, 1))
-        col[3, 0].append((2, 3, 0))
-        col[3, 2].append((2, 3, 2))
-        col[3, 3].append((3, 2, 3))
-        for b in (1, 2, 3):
-            for q in (1, 2, 3):
-                if q != b:
-                    self.down[(b, b), b ^ q] = [0]
-        a, b, _ = self.passes
-        a[1, 0] = [(2, 0, 2, 0, 1), (3, 0, 3, 0, 1), (2, 1, 2, 0, 0), (3, 1, 3, 0, 0)]
-        a[3, 2] = [(3, 2, 3, 3, 1)]
-        a[0, 2] = [(2, 1, 2, 2, 1)]
-        a[0, 3] = [(3, 1, 3, 3, 1)]
-        b[0, 2] = [(3, 1, 2, 3, 1)]
-        b[0, 3] = [(2, 1, 3, 2, 1)]
-        b[1, 3] = [(1, 2, 3, 1, 1)]
-        order = self.order
-        order[0, 1] = [1, 3, 0, 2]
-        order[0, 2] = [2, 3, 0, 1]
-        order[0, 3] = [3, 2, 0, 1]
-        order[1, 2] = [2, 1, 0, 3]
-        order[1, 3] = [1, 3, 0, 2]
-        order[2, 3] = [2, 0, 3, 1]
+                self.row[0][z, c] = [t for t in sorted(range(z, n), key=lambda t: t ^ c) if t != c]
+                self.col[0][z, c] = [(t, z, c) for t in range(z)]
+        waited = {chip: {op[0] for stage in self.step for op in stage.get(chip, []) if op[4]} for chip in chips}
+        order = {chip: self.order.get(chip, list(range(n))) for chip in chips}
+        self.order = order
+        self.waits = {chip: [int(q not in waited[chip]) for q in order[chip]] for chip in chips}
 
     def table(self, get):
         n = self.n
@@ -103,9 +77,10 @@
 
 def kernel(
     n_rcv, n_src, mask_ref, piece_ref, refl_ref, focal_ref,
-    a_buf, gr, gc, y, acc, focal, slab, arrived,
+    a_buf, gr, gc, y, acc, focal, slab, pair, arrived,
     load_sem, own_sem, row_send, pass_send, relay_send, gr_recv,
     col_send, down_send, step_send, gc_recv, gc_local, slab_send, slab_recv,
+    pair_send, pair_recv,
 ):
     n_dev = n_rcv * n_src
     n = n_src // 2
@@ -169,11 +144,11 @@
 
     pl.semaphore_wait(barrier, n_dev - 1)
 
-    def row_to(i):
-        to = look(entry(plan.row, i))
+    def row_to(point, i):
+        to = look(entry(plan.row[point], i))
         slot = 2 * xor(c, to, n) + h
         return to >= 0, pltpu.make_async_remote_copy(
-            src_ref=piece_ref, dst_ref=gr.at[slot], send_sem=row_send.at[i], recv_sem=gr_recv.at[slot],
+            src_ref=piece_ref, dst_ref=gr.at[slot], send_sem=row_send.at[point, i], recv_sem=gr_recv.at[slot],
             device_id=(r, 2 * to + h), device_id_type=MESH,
         )
 
@@ -207,13 +182,14 @@
     def col_part(ref_slot, half):
         return gc.at[ref_slot, :, pl.ds(pl.multiple_of(half * own_p, own_p), own_p), :]
 
-    def col_to(i, k):
-        z = look(entry(plan.col, i, 0))
-        to = look(entry(plan.col, i, 1))
-        slot = look(entry(plan.col, i, 2))
+    def col_to(point, i, k):
+        lists = plan.col[point]
+        z = look(entry(lists, i, 0))
+        to = look(entry(lists, i, 1))
+        slot = look(entry(lists, i, 2))
         return z >= 0, pltpu.make_async_remote_copy(
             src_ref=piece_ref.at[:, :, pl.ds(k * cols, cols)], dst_ref=col_part(slot, h),
-            send_sem=col_send.at[i, k], recv_sem=gc_recv.at[2 * slot + h],
+            send_sem=col_send.at[point, i, k], recv_sem=gc_recv.at[2 * slot + h],
             device_id=(z, 2 * to + k), device_id_type=MESH,
         )
 
@@ -231,7 +207,7 @@
         return width({key: ops for key, ops in plan.down.items() if key[1] == j})
 
     def step_to(stage, i, half):
-        lists = plan.passes[stage]
+        lists = plan.step[stage]
         slot = look(entry(lists, i, 0))
         there = look(entry(lists, i, 3))
         return slot >= 0, look(entry(lists, i, 4)) == 1, slot, pltpu.make_async_remote_copy(
@@ -243,7 +219,7 @@
     def col_arrival(slot, half):
         return pltpu.make_async_remote_copy(
             src_ref=piece_ref.at[:, :, pl.ds(0, cols)], dst_ref=col_part(slot, half),
-            send_sem=col_send.at[0, 0], recv_sem=gc_recv.at[2 * slot + half],
+            send_sem=col_send.at[0, 0, 0], recv_sem=gc_recv.at[2 * slot + half],
             device_id=(r, 2 * c + 1 - h), device_id_type=MESH,
         )
 
@@ -255,7 +231,7 @@
         )
 
     def pass_on(stage):
-        for i in range(width(plan.passes[stage])):
+        for i in range(width(plan.step[stage])):
             for half in range(2):
                 valid, waits, slot, copy = step_to(stage, i, half)
 
@@ -271,39 +247,41 @@
     def _():
         to_partner(0).start()
 
-    for i in range(width(plan.row)):
-        valid, copy = row_to(i)
-        pl.when(valid)(copy.start)
-    for i in range(width(plan.col)):
-        for k in range(2):
-            valid, copy = col_to(i, k)
+    def own_sends(point):
+        ops = [row_to(point, i) for i in range(width(plan.row[point]))]
+        return ops + [col_to(point, i, k) for i in range(width(plan.col[point])) for k in range(2)]
+
+    def begin(point):
+        for valid, copy in own_sends(point):
             pl.when(valid)(copy.start)
 
+    def drained(point):
+        later = plan.row[point + 1], plan.col[point + 1]
+        return look(lambda chip: int(chip[1] < chip[0] and any(lists.get(chip) for lists in later))) == 1
+
+    begin(0)
+
     @pl.when(user)
     def _():
         own_copy.wait()
 
     def take(j):
-        @pl.when(user)
-        def _():
-            arrival(2 * j + h).wait_recv()
-            to_partner(j).start()
-            for i in range(relays(j)):
-                valid, copy = relay_to(j, i)
+        arrival(2 * j + h).wait_recv()
+        to_partner(j).start()
+        for i in range(relays(j)):
+            valid, copy = relay_to(j, i)
+            pl.when(valid)(copy.start)
+
+    def twin(j):
+        arrival(2 * j + 1 - h).wait_recv()
+        for half in range(2):
+            for i in range(downs(j)):
+                valid, copy = down_to(j, i, half)
                 pl.when(valid)(copy.start)
 
-    def twin(j):
-        @pl.when(user)
-        def _():
-            arrival(2 * j + 1 - h).wait_recv()
-            for half in range(2):
-                for i in range(downs(j)):
-                    valid, copy = down_to(j, i, half)
-                    pl.when(valid)(copy.start)
-
-                @pl.when(on_diag)
-                def _():
-                    to_local(j, half).start()
+            @pl.when(on_diag)
+            def _():
+                to_local(j, half).start()
 
     step_rows = min(rows, 1024)
     step_tiles = step_rows // TILE
@@ -391,12 +369,16 @@
     for stage, group in enumerate(groups):
         if stage:
             for j in group:
-                take(j)
-        if stage:
+                pl.when(user)(functools.partial(take, j))
+                pl.when(on_diag)(functools.partial(twin, j))
+            for valid, copy in own_sends(stage - 1):
+                pl.when(valid & drained(stage - 1))(copy.wait_send)
+            begin(stage)
             pass_on(stage - 1)
         for j in group:
-            twin(j)
+            pl.when(full if stage else user)(functools.partial(twin, j))
         first(group[0], len(group))
+    pass_on(2)
 
     for part in range(2):
         @pl.when(user)
@@ -450,68 +432,102 @@
         def _(q):
             second(q, False, True)
 
+    share = n_dev // 2
+    group = max(16, out_rows)
+    each = group // out_rows
+    n_groups = n_p // group // 2
+
+    def rows_of(half, g):
+        return pl.ds(pl.multiple_of((half * n_groups + g) * group, group), group)
+
+    def slab_pair(start):
+        return pltpu.make_async_remote_copy(
+            src_ref=slab.at[pl.ds(start, share)], dst_ref=pair, send_sem=pair_send, recv_sem=pair_recv,
+            device_id=(r, 2 * c + 1 - h), device_id_type=MESH,
+        )
+
+    def slab_to(i):
+        other = h * share + i
+        return pltpu.make_async_remote_copy(
+            src_ref=slab.at[other], dst_ref=arrived.at[chip], send_sem=slab_send.at[i],
+            recv_sem=slab_recv.at[chip],
+            device_id=(other // n_src, lax.rem(other, n_src)), device_id_type=MESH,
+        )
+
+    def slab_from(z, b):
+        return pltpu.make_async_remote_copy(
+            src_ref=slab.at[0], dst_ref=arrived.at[z * n + b], send_sem=slab_send.at[0],
+            recv_sem=slab_recv.at[z * n + b], device_id=(z, 2 * b + me // share), device_id_type=MESH,
+        )
+
     @pl.when(user)
     def _():
-        group = max(16, out_rows)
-
-        @pl.loop(0, n_p // group)
+        @pl.loop(0, n_groups)
         def _(g):
-            at = pl.ds(pl.multiple_of(g * group, group), group)
             for part in range(2):
-                block = focal[part, at, :]
-                for j in range(group // out_rows):
-                    slab[g * (group // out_rows) + j, :, part * n_p:(part + 1) * n_p] = block[
+                block = focal[part, rows_of(1 - h, g), :]
+                for j in range(each):
+                    slab[(1 - h) * share + g * each + j, :, part * n_p:(part + 1) * n_p] = block[
                         j * out_rows:(j + 1) * out_rows
                     ].astype(bf16)
 
-    def slab_to(other):
-        return pltpu.make_async_remote_copy(
-            src_ref=slab.at[other], dst_ref=arrived.at[me], send_sem=slab_send.at[other],
-            recv_sem=slab_recv.at[me],
-            device_id=(other // n_src, lax.rem(other, n_src)), device_id_type=MESH,
-        )
-
-    def slab_from(other):
-        return pltpu.make_async_remote_copy(
-            src_ref=slab.at[me], dst_ref=arrived.at[other], send_sem=slab_send.at[other],
-            recv_sem=slab_recv.at[other],
-            device_id=(other // n_src, lax.rem(other, n_src)), device_id_type=MESH,
-        )
+        slab_pair((1 - h) * share).start()
+        slab_pair(0).wait_recv()
+
+        def begin_slab(i):
+            @pl.when(h * share + i != me)
+            def _():
+                slab_to(i).start()
+
+        @pl.loop(0, n_groups)
+        def _(g):
+            for part in range(2):
+                block = focal[part, rows_of(h, g), :]
+                for j in range(each):
+                    at = slice(part * n_p, (part + 1) * n_p)
+                    slab[h * share + g * each + j, :, at] = (
+                        block[j * out_rows:(j + 1) * out_rows] + pair[g * each + j, :, at].astype(f32)
+                    ).astype(bf16)
+
+            @pl.when(g > 0)
+            def _():
+                for j in range(each):
+                    begin_slab((g - 1) * each + j)
+
+        for j in range(each):
+            begin_slab(share - each + j)
+
+    focal_ref[...] = jnp.zeros_like(focal_ref)
+    own_half = h == me // share
+
+    @pl.when(user & own_half)
+    def _():
+        focal_ref[...] = slab[me].astype(f32)
+
+    for z in range(n):
+        for b in range(z, n):
+            @pl.when(jnp.logical_not(own_half & (chip == z * n + b)))
+            def _():
+                slab_from(z, b).wait_recv()
+                focal_ref[...] += arrived[z * n + b].astype(f32)
 
     @pl.when(user)
     def _():
-        @pl.loop(1, n_dev)
+        slab_pair((1 - h) * share).wait_send()
+
+        @pl.loop(0, share)
         def _(i):
-            slab_to(lax.rem(me + i, n_dev)).start()
-
-    focal_ref[...] = jnp.zeros_like(focal_ref)
-
-    @pl.when(user)
-    def _():
-        focal_ref[...] = slab[me].astype(f32)
-
-    for other in range(n_dev):
-        if (other % n_src) // 2 >= other // n_src:
-            @pl.when(me != other)
+            @pl.when(h * share + i != me)
             def _():
-                slab_from(other).wait_recv()
-                focal_ref[...] += arrived[other].astype(f32)
-
-    @pl.when(user)
-    def _():
-        @pl.loop(1, n_dev)
-        def _(i):
-            slab_to(lax.rem(me + i, n_dev)).wait_send()
-
-    for i in range(width(plan.row)):
-        valid, copy = row_to(i)
-        pl.when(valid)(copy.wait_send)
-    for i in range(width(plan.col)):
-        for k in range(2):
-            valid, copy = col_to(i, k)
+                slab_to(i).wait_send()
+
+    for point in range(3):
+        for valid, copy in own_sends(point):
+            if point < 2:
+                valid = valid & jnp.logical_not(drained(point))
             pl.when(valid)(copy.wait_send)
-    for stage in range(len(plan.passes)):
-        for i in range(width(plan.passes[stage])):
+    for stage in range(3):
+        for i in range(width(plan.step[stage])):
             for half in range(2):
                 valid, _, _, copy = step_to(stage, i, half)
                 pl.when(valid)(copy.wait_send)
@@ -557,9 +573,11 @@
             pltpu.VMEM((2, 4 * own_p * max(2, n - 3), TILE), f32),
             pltpu.VMEM((2, n_p, n_p), f32),
             pltpu.VMEM((n_dev, out_rows, 2 * n_p), bf16),
-            pltpu.VMEM((n_dev, out_rows, 2 * n_p), bf16),
-            dma((n_tiles,)), dma, dma((n,)), dma((n,)), dma((n, 2)), dma((n_src,)),
-            dma((n, 2)), dma((n, 1, 2)), dma((3, 4, 2)), dma((n_src,)), dma((n, 2)), dma((n_dev,)), dma((n_dev,)),
+            pltpu.VMEM((n_dev // 2, out_rows, 2 * n_p), bf16),
+            pltpu.VMEM((n_dev // 2, out_rows, 2 * n_p), bf16),
+            dma((n_tiles,)), dma, dma((3, n)), dma((n,)), dma((n, n)), dma((n_src,)),
+            dma((3, 2 * n, 2)), dma((n, n, 2)), dma((3, 2 * n, 2)), dma((n_src,)), dma((n, 2)), dma((n_dev // 2,)), dma((n_dev // 2,)),
+            dma, dma,
         ],
         compiler_params=pltpu.CompilerParams(
             collective_id=0, has_side_effects=True, vmem_limit_bytes=63 * 1024 * 1024

time: 154 us -> 142 us (0.922)
  Pallas kernels: 150 us -> 138 us
    pallas_call x1, Pallas kernels: 150 us -> 138 us  [body(): pl.pallas_call(functools.partial(kernel, n_rcv, n_src), out_shape=jax.Sha...]
where the time goes in v2:
time: 142 us
  Pallas kernels  138 us (97%)
  local copies, waits for them, and re-layouts  2.07 us (1%)
  other arithmetic  1.82 us (1%)
    pallas_call x1, Pallas kernels, body(): pl.pallas_call(functools.partial(kernel, n_rcv, n_src), out_shape=jax.Sha...  138 us

profile of v2, /device:TPU:13, one launch (start us, length us, event | category | flops | bytes accessed | tf_op | source)
XLA Modules:
  0.0 142.0 jit_solution(17771466672427053066)
XLA Ops:
  0.0 0.0 copy-start
  0.0 1.4 dynamic_slice.3.mask_ref
  1.4 138.1 %focus.1 = f32[16,1024]{1,0:T(8,128)} custom-call(s32[16,8]{1,0:T(8,128)} %dynamic_slice.3.mask_ref, bf16[2,64,4096]{2,1,0:T(8,128)(2,1)} %bitcast.5, bf16[2,4096,2048]{2,1,0:T(8,128)(2,1)} %refl_ref.1), custom_call_target="tpu_custom_call" | custom-call | tf_op jit(solution)/shard_map/focus/pallas_call | solution.py:563
  139.5 0.0 copy-done
  139.5 1.0 select_reduce_fusion.1
  140.4 0.9 add_bitcast_fusion
  141.3 0.7 copy.5
  (1 shorter events, 0.0 us)
Async XLA Ops:
  0.0 139.5 %copy-start = (s32[16]{0:T(128)S(1)}, s32[16]{0:T(128)}, u32[]{:S(2)}) copy-start(s32[16]{0:T(128)} %param.7) | copy-start | bytes 196

commit v3 on v2

--- a/solution.py
+++ b/solution.py
@@ -27,8 +27,8 @@
     {},
 ]
 COL = [
-    {(1, 0): [(0, 1, 0)], (1, 1): [(0, 1, 1)], (2, 0): [(1, 0, 0)], (2, 1): [(1, 2, 1)], (2, 2): [(0, 2, 2)], (3, 0): [(1, 0, 1), (2, 3, 0)], (3, 1): [(1, 3, 1)], (3, 2): [(2, 3, 2)], (3, 3): [(0, 3, 3), (3, 2, 0)]},
-    {},
+    {(1, 1): [(0, 1, 1)], (2, 0): [(1, 0, 0)], (2, 2): [(0, 2, 2)], (3, 0): [(1, 0, 1)], (3, 3): [(0, 3, 3), (3, 2, 0)]},
+    {(1, 0): [(0, 1, 0)], (2, 1): [(1, 2, 1)], (3, 0): [(2, 3, 0)], (3, 1): [(1, 3, 1)], (3, 2): [(2, 3, 2)]},
     {},
 ]
 RELAY = {((0, 1), 2): [0], ((0, 2), 2): [3], ((0, 3), 2): [2], ((0, 3), 1): [1], ((1, 2), 2): [3], ((1, 3), 2): [2], ((1, 3), 1): [1]}
@@ -38,7 +38,8 @@
     {(0, 2): [(3, 1, 2, 3, 1)], (0, 3): [(2, 1, 3, 2, 1)], (1, 3): [(1, 2, 3, 1, 1)]},
     {},
 ]
-ORDER = {(0, 1): [1, 0, 3, 2], (0, 2): [2, 3, 0, 1], (0, 3): [3, 2, 1, 0], (1, 2): [1, 2, 0, 3], (1, 3): [3, 1, 0, 2], (2, 3): [2, 0, 3, 1]}
+ORDER = {(0, 1): [1, 3, 2, 0], (0, 2): [2, 3, 0, 1], (0, 3): [3, 2, 1, 0], (1, 2): [2, 0, 3, 1], (1, 3): [3, 0, 2, 1], (2, 3): [3, 0, 2, 1]}
+EARLY = [(0, 0), (2, 2), (3, 3)]
 
 
 class Plan:
@@ -46,13 +47,14 @@
         self.n = n
         self.row, self.col, self.step = ([{}, {}, {}] for _ in range(3))
         self.relay, self.down, self.order = {}, {}, {}
+        self.early = []
         chips = [(z, c) for z in range(n) for c in range(n)]
         if n == 4:
             for point in range(3):
                 self.row[point] = ROW[point]
                 self.col[point] = COL[point]
                 self.step[point] = STEP[point]
-            self.relay, self.down, self.order = RELAY, DOWN, ORDER
+            self.relay, self.down, self.order, self.early = RELAY, DOWN, ORDER, EARLY
         else:
             for z, c in chips:
                 self.row[0][z, c] = [t for t in sorted(range(z, n), key=lambda t: t ^ c) if t != c]
@@ -76,8 +78,8 @@
 
 
 def kernel(
-    n_rcv, n_src, mask_ref, piece_ref, refl_ref, focal_ref,
-    a_buf, gr, gc, y, acc, focal, slab, pair, arrived,
+    n_rcv, n_src, mask_ref, index_ref, piece_ref, refl_ref, out_ref,
+    focal_ref, a_buf, d_buf, gr, gc, y, y_diag, acc, focal, slab, pair, arrived,
     load_sem, own_sem, row_send, pass_send, relay_send, gr_recv,
     col_send, down_send, step_send, gc_recv, gc_local, slab_send, slab_recv,
     pair_send, pair_recv,
@@ -286,25 +288,42 @@
     step_rows = min(rows, 1024)
     step_tiles = step_rows // TILE
 
-    def clean(t, first, count):
-        for j in range(first, first + count):
-            m = mask_ref[j, t]
+    def clean(t):
+        @pl.when(on_diag)
+        def _():
+            at = pl.ds(pl.multiple_of((h * n_tiles + t) * TILE, TILE), TILE)
+            m = mask_ref[(r * row_tiles + h * n_tiles) + t, s * n_tiles + t]
+            for z in range(2):
+                tile = a_buf[t, z, at, :]
+                d_buf[t, z] = jnp.where(m == 1, tile, jnp.zeros_like(tile))
+                a_buf[t, z, at, :] = jnp.zeros_like(tile)
+
+        for j in range(row_tiles):
+            m = mask_ref[r * row_tiles + j, s * n_tiles + t]
             at = pl.ds(j * TILE, TILE)
             for z in range(2):
                 tile = a_buf[t, z, at, :]
                 a_buf[t, z, at, :] = jnp.where(m == 1, tile, jnp.zeros_like(tile))
 
-    def focal_rows(j, half):
-        return pl.ds(pl.multiple_of(xor(c, j, n) * quarter + half * own_p, own_p), own_p)
-
-    def keep(z, t, j0, nj, block):
-        at = pl.ds(pl.multiple_of(t * TILE, TILE), TILE)
+    unit = max(quarter, 128)
+    per = unit // quarter
+    n_units = n // per
+
+    def keep(ref, j, z, at, block, start):
         block = block.astype(bf16)
+        inner = xor(c, j, n) % per if per > 1 else 0
+        for half in range(2):
+            for part in range(2):
+                begin = start + (half * 2 + part) * own_p
+                rows_at = pl.ds(pl.multiple_of(inner * quarter + half * own_p, own_p), own_p)
+                ref[z, part, rows_at, at] = block[begin:begin + own_p]
+
+    def columns(t):
+        return pl.ds(pl.multiple_of(t * TILE, TILE), TILE)
+
+    def keep_all(z, t, j0, nj, block):
         for j in range(nj):
-            for half in range(2):
-                for part in range(2):
-                    start = ((j * 2 + half) * 2 + part) * own_p
-                    y[z, part, focal_rows(j0 + j, half), at] = block[start:start + own_p]
+            keep(y.at[(j0 + j) // per], j0 + j, z, columns(t), block, j * 2 * quarter)
 
     def first(j0, nj):
         m_rows = nj * 2 * quarter
@@ -315,10 +334,13 @@
             def _(t):
                 if j0 == 0:
                     load(t).wait()
-                    clean(t, 0, row_tiles)
+                    clean(t)
                 left = gr[2 * j0:2 * (j0 + nj)].reshape(m_rows, rows)
                 for z in range(2):
-                    keep(z, t, j0, nj, dot_nn(left, a_buf[t, z]))
+                    keep_all(z, t, j0, nj, dot_nn(left, a_buf[t, z]))
+
+    def first_diag(j0, nj):
+        m_rows = nj * 2 * quarter
 
         @pl.when(on_diag)
         def _():
@@ -326,7 +348,7 @@
             def _(t):
                 if j0 == 0:
                     load(t).wait()
-                    clean(t, 0, row_tiles)
+                    clean(t)
                 col_end = h * cols + (t + 1) * TILE
                 for k in range(rows // step_rows):
                     def step():
@@ -344,46 +366,106 @@
                     else:
                         pl.when(k * step_rows < col_end)(step)
                 for z in range(2):
-                    keep(z, t, j0, nj, acc[z, :m_rows])
-
-    unit = max(quarter, 128)
-    per = unit // quarter
-
-    def second(i, direct, mirror):
+                    keep_all(z, t, j0, nj, acc[z, :m_rows])
+
+    def second(ref, u, i, mirror):
         g = jnp.concatenate([gc[i * per + k, part] for part in range(2) for k in range(per)], axis=0)
         here = pl.ds(pl.multiple_of(i * unit, unit), unit)
+        at = pl.ds(pl.multiple_of(xor(c // per, u, n_units) * unit, unit), unit)
+        block = dot_nt(ref[...].reshape(4 * unit, cols), g)
         sums, turns = [], []
         for z in range(2):
-            by_re = dot_nt(y[z, 0], g)
-            by_im = dot_nt(y[z, 1], g)
+            by_re = block[2 * z * unit:(2 * z + 1) * unit]
+            by_im = block[(2 * z + 1) * unit:(2 * z + 2) * unit]
             sums.append(by_re[:, :unit] + by_im[:, unit:])
             turns.append(by_re[:, unit:] - by_im[:, :unit])
         for part in range(2):
             turn = turns[0] if part else -turns[1]
-            if direct:
-                focal[part, :, here] += sums[part] + turn
+            focal[part, at, here] += sums[part] + turn
             if mirror:
-                focal[part, here, :] += (sums[part] - turn).T
+                focal[part, here, at] += (sums[part] - turn).T
+
+    def diagonal(u):
+        for t in range(n_tiles):
+            at_r = columns(h * n_tiles + t)
+            for k in range(per):
+                j = u * per + k
+                left = gr[pl.ds(2 * j, 2), :, :, at_r].reshape(2 * quarter, TILE)
+                for z in range(2):
+                    keep(y_diag, j, z, columns(t), dot_nn(left, d_buf[t, z]), 0)
+
+    def unit_there(k):
+        return xor(c // per, k, n_units)
+
+    def pairs(p):
+        for k in range(p + 1):
+            second(y.at[p], p, unit_there(k), True)
+        for u in range(p):
+            second(y.at[u], u, unit_there(p), True)
+
+    def diagonal_part(early):
+        split = n_units - 1
+        ahead = look(lambda chip: int(chip in plan.early)) == 1
+
+        def fill(units, others):
+            @pl.loop(*units)
+            def _(u):
+                diagonal(u)
+                for k in range(*others):
+                    second(y_diag, u, unit_there(k), False)
+
+        if early:
+            pl.when(ahead)(lambda: fill((0, split), (0, split)))
+        else:
+            @pl.when(ahead)
+            def _():
+                fill((0, split), (split, n_units))
+                fill((split, n_units), (0, n_units))
+
+            pl.when(jnp.logical_not(ahead))(lambda: fill((0, n_units), (0, n_units)))
+
+    for part in range(2):
+        @pl.when(user)
+        def _():
+            focal[part] = jnp.zeros_like(focal[part])
+
+    def local_wait(j):
+        for half in range(2):
+            to_local(j, half).wait()
 
     groups = [[0], [1, 2]] + ([list(range(3, n))] if n > 3 else [])
     for stage, group in enumerate(groups):
+        if stage == 2 and per == 1:
+            pl.when(on_diag)(lambda: diagonal_part(True))
+        for j in group:
+            if stage:
+                pl.when(user)(functools.partial(take, j))
+            pl.when(on_diag)(functools.partial(twin, j))
+            if j < group[-1] and per == 1:
+                first_diag(j, 1)
+
+                @pl.when(on_diag)
+                def _():
+                    local_wait(j)
+                    pairs(j)
         if stage:
-            for j in group:
-                pl.when(user)(functools.partial(take, j))
-                pl.when(on_diag)(functools.partial(twin, j))
             for valid, copy in own_sends(stage - 1):
                 pl.when(valid & drained(stage - 1))(copy.wait_send)
             begin(stage)
             pass_on(stage - 1)
         for j in group:
-            pl.when(full if stage else user)(functools.partial(twin, j))
+            pl.when(full)(functools.partial(twin, j))
         first(group[0], len(group))
+        if per == 1:
+            first_diag(group[-1], 1)
+
+            @pl.when(on_diag)
+            def _():
+                local_wait(group[-1])
+                pairs(group[-1])
+        else:
+            first_diag(group[0], len(group))
     pass_on(2)
-
-    for part in range(2):
-        @pl.when(user)
-        def _():
-            focal[part] = jnp.zeros_like(focal[part])
 
     @pl.when(full)
     def _():
@@ -401,36 +483,25 @@
                     col_arrival(slot * per + k, 0).wait_recv()
                     col_arrival(slot * per + k, 1).wait_recv()
 
-            second(slot, True, True)
+            for u in range(n_units):
+                second(y.at[u], u, slot, True)
 
     @pl.when(on_diag)
     def _():
-        for j in range(n):
-            for half in range(2):
-                to_local(j, half).wait()
-
-        @pl.loop(0, n // per)
-        def _(q):
-            second(q, True, False)
-
-        @pl.loop(0, n_tiles)
-        def _(t):
-            row = h * n_tiles + t
-            at_r = pl.ds(pl.multiple_of(row * TILE, TILE), TILE)
-            at_c = pl.ds(pl.multiple_of(t * TILE, TILE), TILE)
-            left = gr[:, :, :, at_r].reshape(2 * n_p, TILE)
-            for z in range(2):
-                term = dot_nn(left, a_buf[t, z, at_r, :])
-                for j in range(n_src):
-                    for part in range(2):
-                        at_p = focal_rows(j // 2, j % 2)
-                        start = (j * 2 + part) * own_p
-                        kept = y[z, part, at_p, at_c].astype(f32) - term[start:start + own_p]
-                        y[z, part, at_p, at_c] = kept.astype(bf16)
-
-        @pl.loop(0, n // per)
-        def _(q):
-            second(q, False, True)
+        if per == 1:
+            diagonal_part(False)
+        else:
+            for j in range(n):
+                local_wait(j)
+
+            @pl.loop(0, n_units)
+            def _(u):
+                diagonal(u)
+
+                @pl.loop(0, n_units)
+                def _(k):
+                    second(y.at[u], u, k, True)
+                    second(y_diag, u, k, False)
 
     share = n_dev // 2
     group = max(16, out_rows)
@@ -510,6 +581,13 @@
             def _():
                 slab_from(z, b).wait_recv()
                 focal_ref[...] += arrived[z * n + b].astype(f32)
+
+    real, imag = focal_ref[:, :n_p], focal_ref[:, n_p:]
+    chosen = lax.broadcasted_iota(jnp.int32, (out_rows, n_p), 1) == index_ref[...]
+    anchor_real = jnp.sum(jnp.where(chosen, real, 0.0), axis=1, keepdims=True)
+    anchor_imag = jnp.sum(jnp.where(chosen, imag, 0.0), axis=1, keepdims=True)
+    out_ref[:, 0, :] = real * anchor_real + imag * anchor_imag
+    out_ref[:, 1, :] = imag * anchor_real - real * anchor_imag
 
     @pl.when(user)
     def _():
@@ -554,22 +632,26 @@
     out_rows = n_p // n_dev
     n = n_src // 2
     assert n == n_rcv and rows == 2 * cols
-    r, s = lax.axis_index("rcv"), lax.axis_index("src")
-    row_tiles, n_tiles = rows // TILE, cols // TILE
-    tile_block = lax.dynamic_slice(tile_mask, (r * row_tiles, s * n_tiles), (row_tiles, n_tiles))
+    n_tiles = cols // TILE
+    unit = max(2 * own_p, 128)
     piece = jnp.swapaxes(green, 1, 2)
     dma = pltpu.SemaphoreType.DMA
     any_spec = pl.BlockSpec(memory_space=pl.ANY)
-    focal = pl.pallas_call(
+    return pl.pallas_call(
         functools.partial(kernel, n_rcv, n_src),
-        out_shape=jax.ShapeDtypeStruct((out_rows, 2 * n_p), f32),
-        in_specs=[pl.BlockSpec(memory_space=pltpu.SMEM), any_spec, any_spec],
+        out_shape=jax.ShapeDtypeStruct((out_rows, 2, n_p), f32),
+        in_specs=[
+            pl.BlockSpec(memory_space=pltpu.SMEM), pl.BlockSpec(memory_space=pltpu.VMEM), any_spec, any_spec,
+        ],
         out_specs=pl.BlockSpec(memory_space=pltpu.VMEM),
         scratch_shapes=[
+            pltpu.VMEM((out_rows, 2 * n_p), f32),
             pltpu.VMEM((n_tiles, 2, rows, TILE), bf16),
+            pltpu.VMEM((n_tiles, 2, TILE, TILE), bf16),
             pltpu.VMEM((n_src, 2, own_p, rows), bf16),
             pltpu.VMEM((n, 2, 2 * own_p, cols), bf16),
-            pltpu.VMEM((2, 2, n_p, cols), bf16),
+            pltpu.VMEM((n_p // unit, 2, 2, unit, cols), bf16),
+            pltpu.VMEM((2, 2, unit, cols), bf16),
             pltpu.VMEM((2, 4 * own_p * max(2, n - 3), TILE), f32),
             pltpu.VMEM((2, n_p, n_p), f32),
             pltpu.VMEM((n_dev, out_rows, 2 * n_p), bf16),
@@ -583,15 +665,7 @@
             collective_id=0, has_side_effects=True, vmem_limit_bytes=63 * 1024 * 1024
         ),
         name="focus",
-    )(tile_block, piece, reflection)
-    focal_real = focal[:, :n_p]
-    focal_imag = focal[:, n_p:]
-    chosen = jnp.arange(n_p)[None, :] == reference_index[:, None]
-    anchor_real = jnp.sum(jnp.where(chosen, focal_real, 0.0), axis=1)[:, None]
-    anchor_imag = jnp.sum(jnp.where(chosen, focal_imag, 0.0), axis=1)[:, None]
-    out_real = focal_real * anchor_real + focal_imag * anchor_imag
-    out_imag = focal_imag * anchor_real - focal_real * anchor_imag
-    return jnp.stack([out_real, out_imag], axis=1)
+    )(tile_mask, reference_index[:, None], piece, reflection)
 
 
 def solution(mesh):

time: 142 us -> 134 us (0.944)
  Pallas kernels: 138 us -> 130 us
  other arithmetic: 1.82 us -> 0 us
    pallas_call x1, Pallas kernels: 138 us -> 130 us  [body(): pl.pallas_call(functools.partial(kernel, n_rcv, n_src), out_shape=jax.Sha...]
    unnamed x2 -> x1, local copies, waits for them, and re-layouts: 0.01 us -> 1.47 us
where the time goes in v3:
time: 134 us; the launch traced here: 133 us
  Pallas kernels  130 us (97%)
  local copies, waits for them, and re-layouts  2.8 us (2%)
    pallas_call x1, Pallas kernels, body(): pl.pallas_call(functools.partial(kernel, n_rcv, n_src), out_shape=jax.Sha...  130 us

profile of v3, /device:TPU:13, one launch (start us, length us, event | category | flops | bytes accessed | tf_op | source)
XLA Modules:
  0.0 133.3 jit_solution(7687406963225414138)
XLA Ops:
  0.0 1.3 copy.5.index_ref
  1.3 130.4 %focus.1 = f32[16,2,512]{2,1,0:T(2,128)} custom-call(s32[64,64]{1,0:T(8,128)} %mask_ref.1, s32[16,1]{1,0:T(8,128)} %copy.5.index_ref, bf16[2,64,4096]{2,1,0:T(8,128)(2,1)} %bitcast.2, bf16[2,4096,2048]{2,1,0:T(8,128)(2,1)} %refl_ref.1), custom_call_target="tpu_custom_call" | custom-call | tf_op jit(solution)/shard_map/focus/pallas_call | solution.py:640
  131.8 1.5 %copy.7 = f32[16,2,512]{2,1,0:T(2,128)} copy(f32[16,2,512]{2,1,0:T(2,128)} %focus.1) | data formatting | bytes 131072

commit v4 on v3

--- a/solution.py
+++ b/solution.py
@@ -22,23 +22,23 @@
 
 
 ROW = [
-    {(0, 0): [1, 2], (0, 1): [0, 3], (0, 2): [3, 0], (0, 3): [2, 1], (1, 0): [1, 2], (1, 1): [3], (1, 2): [3], (1, 3): [2, 1], (2, 0): [2, 3], (2, 1): [3, 2], (2, 2): [3], (2, 3): [2], (3, 0): [3], (3, 1): [3], (3, 2): [3]},
+    {(0, 0): [1, 2], (0, 1): [0, 3], (0, 2): [3, 0], (0, 3): [2, 1], (1, 0): [1, 2], (1, 1): [3], (1, 2): [3], (1, 3): [2, 1], (2, 0): [2], (2, 1): [3], (2, 2): [3], (2, 3): [2], (3, 0): [3], (3, 1): [3], (3, 2): [3]},
     {},
     {},
 ]
 COL = [
-    {(1, 1): [(0, 1, 1)], (2, 0): [(1, 0, 0)], (2, 2): [(0, 2, 2)], (3, 0): [(1, 0, 1)], (3, 3): [(0, 3, 3), (3, 2, 0)]},
-    {(1, 0): [(0, 1, 0)], (2, 1): [(1, 2, 1)], (3, 0): [(2, 3, 0)], (3, 1): [(1, 3, 1)], (3, 2): [(2, 3, 2)]},
+    {(1, 0): [(0, 1, 0)], (1, 1): [(0, 1, 1)], (2, 0): [(1, 0, 0)], (2, 1): [(1, 2, 1)], (2, 2): [(0, 2, 2)], (3, 0): [(1, 0, 1)], (3, 1): [(2, 1, 0)], (3, 3): [(0, 3, 3)]},
+    {(3, 0): [(2, 3, 0)], (3, 1): [(1, 3, 1)], (3, 2): [(2, 3, 2)]},
     {},
 ]
-RELAY = {((0, 1), 2): [0], ((0, 2), 2): [3], ((0, 3), 2): [2], ((0, 3), 1): [1], ((1, 2), 2): [3], ((1, 3), 2): [2], ((1, 3), 1): [1]}
+RELAY = {((0, 1), 2): [0], ((0, 2), 2): [3], ((0, 3), 2): [2], ((0, 3), 1): [1], ((1, 2), 2): [3], ((1, 3), 2): [2], ((1, 3), 1): [1], ((2, 2), 2): [3], ((2, 3), 2): [2]}
 DOWN = {((1, 1), 3): [0], ((1, 1), 2): [0], ((2, 2), 3): [0], ((2, 2), 1): [0], ((3, 3), 2): [0], ((3, 3), 1): [0]}
 STEP = [
-    {(0, 2): [(2, 1, 2, 2, 1)], (0, 3): [(3, 1, 3, 3, 1)], (1, 0): [(0, 0, 2, 0, 1), (0, 1, 2, 0, 0), (1, 0, 3, 0, 1), (1, 1, 3, 0, 0)], (3, 2): [(0, 2, 3, 3, 1)]},
-    {(0, 2): [(3, 1, 2, 3, 1)], (0, 3): [(2, 1, 3, 2, 1)], (1, 3): [(1, 2, 3, 1, 1)]},
+    {(0, 2): [(2, 1, 2, 2, 1)], (0, 3): [(3, 1, 3, 3, 1)], (1, 0): [(0, 0, 2, 0, 1), (0, 1, 2, 0, 0), (1, 0, 3, 0, 1), (1, 1, 3, 0, 0)], (1, 3): [(3, 2, 3, 3, 1)], (2, 1): [(0, 2, 3, 1, 1)]},
+    {(0, 2): [(3, 1, 2, 3, 1)], (0, 3): [(2, 1, 3, 2, 1)]},
     {},
 ]
-ORDER = {(0, 1): [1, 3, 2, 0], (0, 2): [2, 3, 0, 1], (0, 3): [3, 2, 1, 0], (1, 2): [2, 0, 3, 1], (1, 3): [3, 0, 2, 1], (2, 3): [3, 0, 2, 1]}
+ORDER = {(0, 1): [1, 0, 3, 2], (0, 2): [2, 3, 0, 1], (0, 3): [3, 2, 1, 0], (1, 2): [1, 2, 0, 3], (1, 3): [3, 2, 1, 0], (2, 3): [2, 0, 3, 1]}
 EARLY = [(0, 0), (2, 2), (3, 3)]
 
 

time: 134 us -> 120 us (0.90)
  Pallas kernels: 130 us -> 116 us
    pallas_call x1, Pallas kernels: 130 us -> 116 us  [body(): pl.pallas_call(functools.partial(kernel, n_rcv, n_src), out_shape=jax.Sha...]
where the time goes in v4:
time: 120 us; the launch traced here: 119 us
  Pallas kernels  116 us (97%)
  local copies, waits for them, and re-layouts  2.8 us (2%)
    pallas_call x1, Pallas kernels, body(): pl.pallas_call(functools.partial(kernel, n_rcv, n_src), out_shape=jax.Sha...  116 us

profile of v4, /device:TPU:13, one launch (start us, length us, event | category | flops | bytes accessed | tf_op | source)
XLA Modules:
  0.0 118.6 jit_solution(18140465363088040483)
XLA Ops:
  0.0 1.3 %copy.5.index_ref = s32[16,1]{1,0:T(8,128)} copy(s32[16,1]{0,1:T(1,128)} %bitcast.3) | data formatting | bytes 128 | tf_op jit(solution)/shard_map/broadcast_in_dim | solution.py:668
  1.3 115.8 %focus.1 = f32[16,2,512]{2,1,0:T(2,128)} custom-call(s32[64,64]{1,0:T(8,128)} %mask_ref.1, s32[16,1]{1,0:T(8,128)} %copy.5.index_ref, bf16[2,64,4096]{2,1,0:T(8,128)(2,1)} %bitcast.2, bf16[2,4096,2048]{2,1,0:T(8,128)(2,1)} %refl_ref.1), custom_call_target="tpu_custom_call" | custom-call | tf_op jit(solution)/shard_map/focus/pallas_call | solution.py:640
  117.2 1.5 %copy.7 = f32[16,2,512]{2,1,0:T(2,128)} copy(f32[16,2,512]{2,1,0:T(2,128)} %focus.1) | data formatting | bytes 131072

commit v5 on v4

--- a/solution.py
+++ b/solution.py
@@ -22,23 +22,23 @@
 
 
 ROW = [
-    {(0, 0): [1, 2], (0, 1): [0, 3], (0, 2): [3, 0], (0, 3): [2, 1], (1, 0): [1, 2], (1, 1): [3], (1, 2): [3], (1, 3): [2, 1], (2, 0): [2], (2, 1): [3], (2, 2): [3], (2, 3): [2], (3, 0): [3], (3, 1): [3], (3, 2): [3]},
-    {},
+    {(0, 0): [1, 2], (0, 1): [0, 3], (0, 2): [3, 0], (0, 3): [2, 1], (1, 0): [1, 2], (1, 1): [3], (1, 2): [3], (1, 3): [2, 1], (2, 0): [2], (2, 1): [3], (2, 2): [3], (2, 3): [2], (3, 1): [3], (3, 2): [3]},
+    {(3, 0): [3]},
     {},
 ]
 COL = [
-    {(1, 0): [(0, 1, 0)], (1, 1): [(0, 1, 1)], (2, 0): [(1, 0, 0)], (2, 1): [(1, 2, 1)], (2, 2): [(0, 2, 2)], (3, 0): [(1, 0, 1)], (3, 1): [(2, 1, 0)], (3, 3): [(0, 3, 3)]},
-    {(3, 0): [(2, 3, 0)], (3, 1): [(1, 3, 1)], (3, 2): [(2, 3, 2)]},
+    {(1, 0): [(0, 1, 0)], (1, 1): [(0, 1, 1)], (2, 0): [(1, 0, 2)], (2, 1): [(1, 0, 1)], (2, 2): [(0, 2, 2)], (3, 0): [(1, 0, 0)], (3, 1): [(2, 0, 0), (2, 1, 0)], (3, 3): [(0, 3, 3)]},
+    {(3, 2): [(2, 3, 2)]},
     {},
 ]
 RELAY = {((0, 1), 2): [0], ((0, 2), 2): [3], ((0, 3), 2): [2], ((0, 3), 1): [1], ((1, 2), 2): [3], ((1, 3), 2): [2], ((1, 3), 1): [1], ((2, 2), 2): [3], ((2, 3), 2): [2]}
-DOWN = {((1, 1), 3): [0], ((1, 1), 2): [0], ((2, 2), 3): [0], ((2, 2), 1): [0], ((3, 3), 2): [0], ((3, 3), 1): [0]}
+DOWN = {((1, 1), 2): [0], ((1, 1), 3): [0], ((2, 2), 1): [0], ((2, 2), 3): [0], ((3, 3), 2): [0], ((3, 3), 1): [0]}
 STEP = [
-    {(0, 2): [(2, 1, 2, 2, 1)], (0, 3): [(3, 1, 3, 3, 1)], (1, 0): [(0, 0, 2, 0, 1), (0, 1, 2, 0, 0), (1, 0, 3, 0, 1), (1, 1, 3, 0, 0)], (1, 3): [(3, 2, 3, 3, 1)], (2, 1): [(0, 2, 3, 1, 1)]},
-    {(0, 2): [(3, 1, 2, 3, 1)], (0, 3): [(2, 1, 3, 2, 1)]},
+    {(0, 2): [(2, 1, 2, 2, 1)], (0, 3): [(3, 1, 3, 3, 1)], (1, 0): [(0, 1, 3, 0, 1), (1, 1, 2, 1, 1), (2, 0, 2, 0, 1), (0, 0, 3, 0, 0), (2, 1, 2, 0, 0), (0, 2, 3, 0, 0)], (2, 0): [(0, 1, 3, 1, 1)], (2, 1): [(0, 2, 3, 1, 1)]},
+    {(0, 2): [(3, 1, 2, 3, 1)], (0, 3): [(2, 1, 3, 2, 1)], (1, 3): [(3, 2, 3, 3, 1)]},
     {},
 ]
-ORDER = {(0, 1): [1, 0, 3, 2], (0, 2): [2, 3, 0, 1], (0, 3): [3, 2, 1, 0], (1, 2): [1, 2, 0, 3], (1, 3): [3, 2, 1, 0], (2, 3): [2, 0, 3, 1]}
+ORDER = {(0, 1): [1, 0, 3, 2], (0, 2): [2, 3, 0, 1], (0, 3): [3, 2, 1, 0], (1, 2): [2, 1, 0, 3], (1, 3): [0, 3, 1, 2], (2, 3): [2, 0, 3, 1]}
 EARLY = [(0, 0), (2, 2), (3, 3)]
 
 

time: 120 us -> 120 us (level)
  no operation moved by 1% of the time
where the time goes in v5:
time: 120 us; the launch traced here: 118 us
  Pallas kernels  115 us (96%)
  local copies, waits for them, and re-layouts  2.8 us (2%)
    pallas_call x1, Pallas kernels, body(): pl.pallas_call(functools.partial(kernel, n_rcv, n_src), out_shape=jax.Sha...  115 us

profile of v5, /device:TPU:13, one launch (start us, length us, event | category | flops | bytes accessed | tf_op | source)
XLA Modules:
  0.0 118.0 jit_solution(3360514857384301523)
XLA Ops:
  0.0 1.3 %copy.5.index_ref = s32[16,1]{1,0:T(8,128)} copy(s32[16,1]{0,1:T(1,128)} %bitcast.3) | data formatting | bytes 128 | tf_op jit(solution)/shard_map/broadcast_in_dim | solution.py:668
  1.3 115.2 %focus.1 = f32[16,2,512]{2,1,0:T(2,128)} custom-call(s32[64,64]{1,0:T(8,128)} %mask_ref.1, s32[16,1]{1,0:T(8,128)} %copy.5.index_ref, bf16[2,64,4096]{2,1,0:T(8,128)(2,1)} %bitcast.2, bf16[2,4096,2048]{2,1,0:T(8,128)(2,1)} %refl_ref.1), custom_call_target="tpu_custom_call" | custom-call | tf_op jit(solution)/shard_map/focus/pallas_call | solution.py:640
  116.6 1.5 %copy.7 = f32[16,2,512]{2,1,0:T(2,128)} copy(f32[16,2,512]{2,1,0:T(2,128)} %focus.1) | data formatting | bytes 131072
